TPU v7x, 32 devices: a whole 2x2x4 slice. The times are simulated.
32 devices in a mesh: shard: 4 (over z), ctx: 2 (over y), tp: 4 (over x, core).
Axes of the slice: x: 2, y: 2, z: 4, core: 2. Of those that a mesh axis runs over, the one named last changes fastest.
Arguments:
- inputs: float32 [8, 256, 1024], P('shard', 'ctx'), may hold values from -12 to 12
- segment_ids: int32 [8, 256], P('shard', 'ctx'), may hold values from 0 to 3, never falling along the last dimension, each value on 1 to 128 neighbouring positions
- gains: bfloat16 [2, 1024], P(None, ('shard', 'ctx')), may hold values from 0.5 to 1.5
- shifts: bfloat16 [2, 1024], P(None, ('shard', 'ctx')), may hold values from -3 to 3
- attend_weight: bfloat16 [1024, 3, 1024], P(('shard', 'ctx'), None, 'tp'), may hold values from -1 to 1
- merge_weight: bfloat16 [1024, 1024], P(('shard', 'ctx'), 'tp'), may hold values from -0.75 to 0.75
- expand_weight: bfloat16 [1024, 4096], P(('shard', 'ctx'), 'tp'), may hold values from -0.1875 to 0.1875
- expand_bias: bfloat16 [4, 1024], P('tp', ('shard', 'ctx')), may hold values from -3 to 3
- reduce_weight: bfloat16 [1024, 4096], P(('shard', 'ctx'), 'tp'), may hold values from -0.09375 to 0.09375
- cotangent: float32 [8, 256, 1024], P('shard', 'ctx'), may hold values from -6 to 6
Outputs:
- block_out: float32 [8, 256, 1024], P('shard', 'ctx')
- input_grad: float32 [8, 256, 1024], P('shard', 'ctx')
- gains_grad: float32 [2, 1024], P(None, ('shard', 'ctx'))
- shifts_grad: float32 [2, 1024], P(None, ('shard', 'ctx'))
- attend_grad: float32 [1024, 3, 1024], P(('shard', 'ctx'), None, 'tp')
- merge_grad: float32 [1024, 1024], P(('shard', 'ctx'), 'tp')
- expand_grad: float32 [1024, 4096], P(('shard', 'ctx'), 'tp')
- bias_grad: float32 [4, 1024], P('tp', ('shard', 'ctx'))
- reduce_grad: float32 [1024, 4096], P(('shard', 'ctx'), 'tp')
Inputs may be any that keep to these rules, and one draw needn't show every extreme that they name: `segment_ids`: within each sequence segment ids never fall; every document holds 1 to 128 tokens, and one of them exactly 128.
All inputs are finite; a program needn't handle non-finite values.
Results may differ from a plain program's by a relative error of at most 0.0093.
Values may be sent and summed in bfloat16 or wider, within the bound.
No kernel may reach another device: no remote copies, remote signals or barrier semaphores. Data moves between devices by JAX's collectives and lax.ppermute only.
A program may use at most 128 MiB of HBM per device.

v0:
```python
import jax
import jax.numpy as jnp
from jax import lax
from jax.sharding import PartitionSpec as P

HD = 64
epsilon = 1e-05
masked_score = -1e30
gelu_scale = 0.7978845608028654
gelu_cubic = 0.044715


def norm_forward(values, gain, shift):
    average = jnp.mean(values, axis=-1, keepdims=True)
    centered = values - average
    variance = jnp.mean(centered * centered, axis=-1, keepdims=True)
    inverse = lax.rsqrt(variance + epsilon)
    normed = centered * inverse
    return (normed, inverse, normed * gain.astype(jnp.float32) + shift.astype(jnp.float32))


def norm_backward(upstream, normed, inverse, gain):
    scaled = upstream * gain.astype(jnp.float32)
    first_mean = jnp.mean(scaled, axis=-1, keepdims=True)
    second_mean = jnp.mean(scaled * normed, axis=-1, keepdims=True)
    return inverse * (scaled - first_mean - normed * second_mean)


def gelu_pair(pre_act):
    inner_arg = gelu_scale * (pre_act + gelu_cubic * pre_act * pre_act * pre_act)
    tangent = jnp.tanh(inner_arg)
    gelu_value = 0.5 * pre_act * (1.0 + tangent)
    gelu_slope = 0.5 * (1.0 + tangent) + 0.5 * pre_act * (1.0 - tangent * tangent) * gelu_scale * (
        1.0 + 3.0 * gelu_cubic * pre_act * pre_act
    )
    return (gelu_value, gelu_slope)


def shards(
    inputs,
    segment_ids,
    gains,
    shifts,
    attend_weight,
    merge_weight,
    expand_weight,
    expand_bias,
    reduce_weight,
    cotangent,
):
    seq_count, group_len, model_width = inputs.shape
    row_count = seq_count * group_len
    full_len = group_len * lax.axis_size("ctx")
    head_scale = HD ** (-0.5)
    gathered = (
        lax.all_gather(attend_weight, ("shard", "ctx"), axis=0, tiled=True),
        lax.all_gather(merge_weight, ("shard", "ctx"), axis=0, tiled=True),
        lax.all_gather(expand_weight, ("shard", "ctx"), axis=0, tiled=True),
        lax.all_gather(reduce_weight, ("shard", "ctx"), axis=0, tiled=True),
        lax.all_gather(expand_bias, ("shard", "ctx"), axis=1, tiled=True),
        lax.all_gather(gains, ("shard", "ctx"), axis=1, tiled=True),
        lax.all_gather(shifts, ("shard", "ctx"), axis=1, tiled=True),
    )
    attend_full, merge_full, expand_full, reduce_full, bias_full, gains_full, shifts_full = gathered
    local_cols = attend_full.shape[2]
    head_local = local_cols // HD
    flat_in = inputs.reshape(row_count, model_width)
    normed_early, inverse_early, affine_early = norm_forward(flat_in, gains_full[0], shifts_full[0])
    hidden_early = affine_early.astype(jnp.bfloat16)
    projected = jnp.einsum(
        "rd,dtc->rtc", hidden_early, attend_full, preferred_element_type=jnp.float32
    )
    query_heads = (
        (projected[:, 0] * head_scale)
        .astype(jnp.bfloat16)
        .reshape(seq_count, group_len, head_local, HD)
    )
    key_rows = projected[:, 1].astype(jnp.bfloat16).reshape(seq_count, group_len, local_cols)
    value_rows = projected[:, 2].astype(jnp.bfloat16).reshape(seq_count, group_len, local_cols)
    all_keys, all_values, all_segments = (
        lax.all_gather(key_rows, "ctx", axis=1, tiled=True),
        lax.all_gather(value_rows, "ctx", axis=1, tiled=True),
        lax.all_gather(segment_ids, "ctx", axis=1, tiled=True),
    )
    key_heads = all_keys.reshape(seq_count, full_len, head_local, HD)
    value_heads = all_values.reshape(seq_count, full_len, head_local, HD)
    query_pos = lax.axis_index("ctx") * group_len + jnp.arange(group_len, dtype=jnp.int32)
    key_pos = jnp.arange(full_len, dtype=jnp.int32)
    allowed = (segment_ids[:, :, None] == all_segments[:, None, :]) & (
        key_pos[None, None, :] <= query_pos[None, :, None]
    )
    allowed = allowed[:, None]

    def score_block():
        raw_scores = jnp.einsum(
            "sqhd,skhd->shqk", query_heads, key_heads, preferred_element_type=jnp.float32
        )
        return jnp.where(allowed, raw_scores, masked_score)

    scores = score_block()
    row_top = jnp.max(scores, axis=-1, keepdims=True)
    log_total = row_top + jnp.log(jnp.sum(jnp.exp(scores - row_top), axis=-1, keepdims=True))
    attn_probs = jnp.exp(scores - log_total)
    probs_half = attn_probs.astype(jnp.bfloat16)
    attended_heads = jnp.einsum(
        "shqk,skhd->sqhd", probs_half, value_heads, preferred_element_type=jnp.float32
    ).astype(jnp.bfloat16)
    attended = attended_heads.reshape(row_count, local_cols)
    merge_part = jnp.einsum("rc,oc->ro", attended, merge_full, preferred_element_type=jnp.float32)
    residual = flat_in + lax.psum(merge_part, "tp")
    normed_later, inverse_later, affine_later = norm_forward(
        residual, gains_full[1], shifts_full[1]
    )
    hidden_later = affine_later.astype(jnp.bfloat16)
    pre_act = jnp.dot(
        hidden_later, expand_full, preferred_element_type=jnp.float32
    ) + bias_full.astype(jnp.float32)
    gelu_value, gelu_slope = gelu_pair(pre_act)
    activated = gelu_value.astype(jnp.bfloat16)
    reduce_part = jnp.einsum(
        "rf,of->ro", activated, reduce_full, preferred_element_type=jnp.float32
    )
    block_out = residual + lax.psum(reduce_part.astype(jnp.bfloat16), "tp").astype(jnp.float32)
    back_set = (
        lax.all_gather(attend_weight, ("shard", "ctx"), axis=0, tiled=True),
        lax.all_gather(merge_weight, ("shard", "ctx"), axis=0, tiled=True),
        lax.all_gather(expand_weight, ("shard", "ctx"), axis=0, tiled=True),
        lax.all_gather(reduce_weight, ("shard", "ctx"), axis=0, tiled=True),
        lax.all_gather(gains, ("shard", "ctx"), axis=1, tiled=True),
    )
    attend_back, merge_back, expand_back, reduce_back, gains_back = back_set
    output_grad = cotangent.reshape(row_count, model_width)
    cot_half = output_grad.astype(jnp.bfloat16)
    reduce_grad = jnp.einsum("ro,rf->of", cot_half, activated, preferred_element_type=jnp.float32)
    pre_grad = jnp.dot(cot_half, reduce_back, preferred_element_type=jnp.float32) * gelu_slope
    pre_half = pre_grad.astype(jnp.bfloat16)
    bias_grad = jnp.sum(pre_grad, axis=0, keepdims=True)
    expand_grad = jnp.einsum(
        "rd,rf->df", hidden_later, pre_half, preferred_element_type=jnp.float32
    )
    later_part = jnp.einsum("rf,df->rd", pre_half, expand_back, preferred_element_type=jnp.float32)
    later_grad = lax.psum(later_part, "tp")
    residual_grad = output_grad + norm_backward(
        later_grad, normed_later, inverse_later, gains_back[1]
    )
    resid_half = residual_grad.astype(jnp.bfloat16)
    merge_grad = jnp.einsum("ro,rc->oc", resid_half, attended, preferred_element_type=jnp.float32)
    attended_grad = jnp.dot(resid_half, merge_back, preferred_element_type=jnp.float32).astype(
        jnp.bfloat16
    )
    grad_heads = attended_grad.reshape(seq_count, group_len, head_local, HD)
    scores_again = score_block()
    probs_again = jnp.exp(scores_again - log_total)
    probs_again_half = probs_again.astype(jnp.bfloat16)
    row_delta = jnp.einsum(
        "sqhd,sqhd->shq", grad_heads, attended_heads, preferred_element_type=jnp.float32
    )
    prob_grad = jnp.einsum(
        "sqhd,skhd->shqk", grad_heads, value_heads, preferred_element_type=jnp.float32
    )
    score_grad = probs_again * (prob_grad - row_delta[..., None])
    score_half = score_grad.astype(jnp.bfloat16)
    query_grad = (
        jnp.einsum("shqk,skhd->sqhd", score_half, key_heads, preferred_element_type=jnp.float32)
        * head_scale
    )
    keys_part = jnp.einsum(
        "shqk,sqhd->skhd", score_half, query_heads, preferred_element_type=jnp.float32
    ).reshape(seq_count, full_len, local_cols)
    values_part = jnp.einsum(
        "shqk,sqhd->skhd", probs_again_half, grad_heads, preferred_element_type=jnp.float32
    ).reshape(seq_count, full_len, local_cols)
    keys_grad, values_grad = (
        lax.psum_scatter(keys_part, "ctx", scatter_dimension=1, tiled=True),
        lax.psum_scatter(values_part, "ctx", scatter_dimension=1, tiled=True),
    )
    proj_grad = jnp.stack(
        [
            query_grad.reshape(row_count, local_cols),
            keys_grad.reshape(row_count, local_cols),
            values_grad.reshape(row_count, local_cols),
        ],
        axis=1,
    ).astype(jnp.bfloat16)
    attend_grad = jnp.einsum(
        "rd,rtc->dtc", hidden_early, proj_grad, preferred_element_type=jnp.float32
    )
    early_part = jnp.einsum(
        "rtc,dtc->rd", proj_grad, attend_back, preferred_element_type=jnp.float32
    )
    early_grad = lax.psum(early_part, "tp")
    input_grad = residual_grad + norm_backward(
        early_grad, normed_early, inverse_early, gains_back[0]
    )
    gains_grad = jnp.stack(
        [jnp.sum(early_grad * normed_early, axis=0), jnp.sum(later_grad * normed_later, axis=0)]
    )
    shifts_grad = jnp.stack([jnp.sum(early_grad, axis=0), jnp.sum(later_grad, axis=0)])
    shares = (
        lax.psum_scatter(attend_grad, ("shard", "ctx"), scatter_dimension=0, tiled=True),
        lax.psum_scatter(merge_grad, ("shard", "ctx"), scatter_dimension=0, tiled=True),
        lax.psum_scatter(expand_grad, ("shard", "ctx"), scatter_dimension=0, tiled=True),
        lax.psum_scatter(reduce_grad, ("shard", "ctx"), scatter_dimension=0, tiled=True),
        lax.psum_scatter(bias_grad, ("shard", "ctx"), scatter_dimension=1, tiled=True),
        lax.psum_scatter(gains_grad, ("shard", "ctx"), scatter_dimension=1, tiled=True),
        lax.psum_scatter(shifts_grad, ("shard", "ctx"), scatter_dimension=1, tiled=True),
    )
    return (
        block_out.reshape(inputs.shape),
        input_grad.reshape(inputs.shape),
        shares[5],
        shares[6],
        shares[0],
        shares[1],
        shares[2],
        shares[4],
        shares[3],
    )


def solution(mesh):
    in_specs = (
        P("shard", "ctx", None),
        P("shard", "ctx"),
        P(None, ("shard", "ctx")),
        P(None, ("shard", "ctx")),
        P(("shard", "ctx"), None, "tp"),
        P(("shard", "ctx"), "tp"),
        P(("shard", "ctx"), "tp"),
        P("tp", ("shard", "ctx")),
        P(("shard", "ctx"), "tp"),
        P("shard", "ctx", None),
    )
    out_specs = (
        P("shard", "ctx", None),
        P("shard", "ctx", None),
        P(None, ("shard", "ctx")),
        P(None, ("shard", "ctx")),
        P(("shard", "ctx"), None, "tp"),
        P(("shard", "ctx"), "tp"),
        P(("shard", "ctx"), "tp"),
        P("tp", ("shard", "ctx")),
        P(("shard", "ctx"), "tp"),
    )
    return jax.shard_map(shards, mesh=mesh, in_specs=in_specs, out_specs=out_specs, check_vma=False)
```

profile of v0, /device:TPU:0, one launch (start us, length us, event | category | flops | bytes accessed | tf_op | source)
XLA Modules:
  0.0 930.5 jit_solution(1876446625818564370)
XLA Ops:
  8.0 1.4 reduce_sum.126
  9.4 5.5 all_gather.39
  14.8 21.4 %all_gather.35 = bf16[2,1024]{1,0:T(2,128)(2,1)S(1)} all-gather(bf16[2,128]{1,0:T(2,128)(2,1)} %param.12), channel_id=1, replica_groups=mesh['shard'=4,'ctx'=2,'tp'=4] {'shard','ctx'}, dimensions={1}, use_global_device_ids=true | all-gather | bytes 4608 | tf_op jit(solution)/shard_map/all_gather | solution.py:61
  36.3 16.5 %all_gather.36 = bf16[2,1024]{1,0:T(2,128)(2,1)S(1)} all-gather(bf16[2,128]{1,0:T(2,128)(2,1)} %param.13), channel_id=1, replica_groups=mesh['shard'=4,'ctx'=2,'tp'=4] {'shard','ctx'}, dimensions={1}, use_global_device_ids=true | all-gather | bytes 4608 | tf_op jit(solution)/shard_map/all_gather | solution.py:62
  52.8 1.5 multiply_reduce_fusion.5
  54.6 31.4 %all_gather.41 = bf16[1024,256]{1,0:T(8,128)(2,1)S(1)} all-gather(bf16[128,256]{1,0:T(8,128)(2,1)S(1)} %copy-done.16), channel_id=1, replica_groups=mesh['shard'=4,'ctx'=2,'tp'=4] {'shard','ctx'}, dimensions={0}, use_global_device_ids=true | all-gather | bytes 589824 | tf_op jit(solution)/shard_map/all_gather | solution.py:57
  86.3 2.1 fusion.38
  88.5 5.6 all_gather.38
  95.0 5.6 all_gather.40
  105.7 18.4 %all_gather.43 = bf16[1,1024]{1,0:T(2,128)(2,1)S(1)} all-gather(bf16[1,128]{1,0:T(2,128)(2,1)S(1)} %copy-done.31), channel_id=1, replica_groups=mesh['shard'=4,'ctx'=2,'tp'=4] {'shard','ctx'}, dimensions={1}, use_global_device_ids=true | all-gather | bytes 2304 | tf_op jit(solution)/shard_map/all_gather | solution.py:60
  124.2 2.1 bitcast_convert_fusion
  126.3 13.4 %all-reduce.5.cloned.1.call-done = f32[256,1024]{1,0:T(8,128)} async-done(((f32[256,1024]{1,0:T(8,128)}), f32[256,1024]{1,0:T(8,128)}) %all-reduce.5.cloned.1.call-update) | async-done | bytes 1048592 | tf_op jit(solution)/shard_map/psum | solution.py:110
  139.6 1.4 fusion.36
  141.3 50.0 %all-gather.6.cloned.1.call-done = bf16[1024,1024]{1,0:T(8,128)(2,1)} async-done(((bf16[128,1024]{1,0:T(8,128)(2,1)}), bf16[1024,1024]{1,0:T(8,128)(2,1)}) %all-gather.6.cloned.1.call-update) | async-done | bytes 2097168 | tf_op jit(solution)/shard_map/all_gather | solution.py:58
  191.4 3.3 convolution_add_fusion
  194.7 46.3 %all-gather.8.cloned.1.call-done = bf16[1024,1024]{1,0:T(8,128)(2,1)} async-done(((bf16[128,1024]{1,0:T(8,128)(2,1)}), bf16[1024,1024]{1,0:T(8,128)(2,1)}) %all-gather.8.cloned.1.call-update) | async-done | bytes 2097168 | tf_op jit(solution)/shard_map/all_gather | solution.py:59
  241.0 3.9 fusion.40
  245.7 1.7 fusion.21
  247.5 3.5 convolution_convert_fusion
  251.1 31.3 %all-reduce.9.cloned.1.call-done = f32[256,1024]{1,0:T(8,128)} async-done(((f32[256,1024]{1,0:T(8,128)}), f32[256,1024]{1,0:T(8,128)}) %all-reduce.9.cloned.1.call-update) | async-done | bytes 1048592 | tf_op jit(solution)/shard_map/psum | solution.py:142
  282.4 2.3 multiply_reduce_fusion
  284.8 34.3 %all-reduce.7.cloned.1.call-done = bf16[256,1024]{1,0:T(8,128)(2,1)} async-done(((bf16[256,1024]{1,0:T(8,128)(2,1)}), bf16[256,1024]{1,0:T(8,128)(2,1)}) %all-reduce.7.cloned.1.call-update) | async-done | bytes 524304 | tf_op jit(solution)/shard_map/psum | solution.py:123
  319.1 3.0 bitcast_add_fusion
  327.5 1.4 fusion.1
  330.8 1.3 fusion.3
  332.5 8.7 reduce-scatter.18.cloned.1.call-done
  342.3 15.8 %reduce-scatter.16.cloned.1.call-done = f32[2,128,256]{1,2,0:T(8,128)} async-done(((f32[2,256,256]{1,2,0:T(8,128)}), f32[2,128,256]{1,2,0:T(8,128)}) %reduce-scatter.16.cloned.1.call-update) | async-done | bytes 262160 | tf_op jit(solution)/shard_map/reduce_scatter | solution.py:174
  359.2 3.0 convolution_bitcast_fusion.1
  363.6 35.1 %all-reduce.11.cloned.1.call-done = f32[256,1024]{1,0:T(8,128)} async-done(((f32[256,1024]{1,0:T(8,128)}), f32[256,1024]{1,0:T(8,128)}) %all-reduce.11.cloned.1.call-update) | async-done | bytes 1048592 | tf_op jit(solution)/shard_map/psum | solution.py:191
  398.7 2.5 multiply_reduce_fusion.1
  401.8 1.7 copy.70
  404.9 1.7 copy.68
  406.7 3.9 convolution_bitcast_fusion
  411.8 2.3 fusion.16
  414.1 3.4 fusion.11
  418.2 3.9 fusion.19
  422.2 42.8 %reduce-scatter.32.cloned.1.call-done = f32[128,1]{1,0:T(8,128)} async-done(((f32[1024,1]{1,0:T(8,128)}), f32[128,1]{1,0:T(8,128)}) %reduce-scatter.32.cloned.1.call-update) | async-done | bytes 528
  465.0 1.4 copy.73
  466.5 1.3 multiply_add_fusion.1
  467.8 62.1 %reduce-scatter.30.cloned.1.call-done = f32[128,2]{1,0:T(8,128)} async-done(((f32[1024,2]{1,0:T(8,128)}), f32[128,2]{1,0:T(8,128)}) %reduce-scatter.30.cloned.1.call-update) | async-done | bytes 1040
  530.0 1.5 copy.71
  531.4 63.9 %reduce-scatter.28.cloned.1.call-done = f32[128,2]{1,0:T(8,128)} async-done(((f32[1024,2]{1,0:T(8,128)}), f32[128,2]{1,0:T(8,128)}) %reduce-scatter.28.cloned.1.call-update) | async-done | bytes 1040
  595.4 1.5 copy.69
  596.8 89.8 %reduce-scatter.26.cloned.1.call-done = f32[128,1024]{0,1:T(8,128)} async-done(((f32[1024,1024]{0,1:T(8,128)}), f32[128,1024]{0,1:T(8,128)}) %reduce-scatter.26.cloned.1.call-update) | async-done | bytes 524304 | tf_op jit(solution)/shard_map/reduce_scatter | solution.py:203
  686.7 2.0 copy.58
  688.7 65.8 %reduce-scatter.22.cloned.1.call-done = f32[128,256]{1,0:T(8,128)} async-done(((f32[1024,256]{1,0:T(8,128)}), f32[128,256]{1,0:T(8,128)}) %reduce-scatter.22.cloned.1.call-update) | async-done | bytes 131088 | tf_op jit(solution)/shard_map/reduce_scatter | solution.py:201
  754.5 78.0 %reduce-scatter.20.cloned.1.call-done = f32[128,3,256]{2,0,1:T(8,128)} async-done(((f32[1024,3,256]{2,0,1:T(8,128)}), f32[128,3,256]{2,0,1:T(8,128)}) %reduce-scatter.20.cloned.1.call-update) | async-done | bytes 393232 | tf_op jit(solution)/shard_map/reduce_scatter | solution.py:200
  832.4 91.5 %reduce-scatter.24.cloned.1.call-done = f32[128,1024]{1,0:T(8,128)} async-done(((f32[1024,1024]{1,0:T(8,128)}), f32[128,1024]{1,0:T(8,128)}) %reduce-scatter.24.cloned.1.call-update) | async-done | bytes 524304 | tf_op jit(solution)/shard_map/reduce_scatter | solution.py:202
  (140 shorter events, 23.3 us)
Async XLA Ops:
  7.2 78.8 %copy-start = (f32[2,128,1024]{2,1,0:T(8,128)S(1)}, f32[2,128,1024]{2,1,0:T(8,128)}, u32[]{:S(2)}) copy-start(f32[2,128,1024]{2,1,0:T(8,128)} %param.10) | copy-start | bytes 3145732
  7.2 47.3 %copy-start.28 = (s32[2,128]{1,0:T(2,128)S(1)}, s32[2,128]{1,0:T(2,128)}, u32[]{:S(2)}) copy-start(s32[2,128]{1,0:T(2,128)} %param.11) | copy-start | bytes 3076
  7.2 47.4 %copy-start.16 = (bf16[128,256]{1,0:T(8,128)(2,1)S(1)}, bf16[128,256]{1,0:T(8,128)(2,1)}, u32[]{:S(2)}) copy-start(bf16[128,256]{1,0:T(8,128)(2,1)} %param.15) | copy-start | bytes 196612
  7.2 79.1 %all-gather.4.cloned.1.call-start = ((), (), s32[]{:S(2)}) async-start(), calls=%async_computation.9 | async-start | bytes 1769472 | tf_op jit(solution)/shard_map/all_gather | solution.py:56
  7.9 131.7 %all-reduce.5.cloned.1.call-start = ((), (), s32[]{:S(2)}) async-start(), calls=%async_computation.10 | async-start | bytes 2097152 | tf_op jit(solution)/shard_map/psum | solution.py:110
  52.8 35.6 %copy-start.21 = (f32[256]{0:T(256)}, f32[256]{0:T(256)S(1)}, u32[]{:S(2)}) copy-start(f32[256]{0:T(256)S(1)} %get-tuple-element.54) | copy-start | bytes 3076
  54.3 34.1 %copy-start.23 = (f32[256]{0:T(256)}, f32[256]{0:T(256)S(1)}, u32[]{:S(2)}) copy-start(f32[256]{0:T(256)S(1)} %rsqrt_bitcast_fusion) | copy-start | bytes 3076
  54.4 137.0 %copy-start.19 = (f32[1,1024]{1,0:T(1,128)}, f32[1,1024]{1,0:T(1,128)S(1)}, u32[]{:S(2)}) copy-start(f32[1,1024]{1,0:T(1,128)S(1)} %get-tuple-element.52) | copy-start | bytes 12292
  86.0 16.5 %copy-start.3 = (bf16[1024,256]{1,0:T(8,128)(2,1)}, bf16[1024,256]{1,0:T(8,128)(2,1)S(1)}, u32[]{:S(2)}) copy-start(bf16[1024,256]{1,0:T(8,128)(2,1)S(1)} %all_gather.41) | copy-start | bytes 1572868
  86.2 7.9 copy-start.6
  100.6 1.3 copy-start.9
  101.1 1.4 copy-start.12
  102.3 0.7 copy-start.15
  102.3 3.4 copy-start.31
  102.5 23.8 %copy-start.14 = (bf16[2,128,4,64]{1,0,3,2:T(2,128)(2,1)}, bf16[2,128,4,64]{1,0,3,2:T(2,128)(2,1)S(1)}, u32[]{:S(2)}) copy-start(bf16[2,128,4,64]{1,0,3,2:T(2,128)(2,1)S(1)} %copy.48) | copy-start | bytes 393220
  104.3 87.0 %all-gather.6.cloned.1.call-start = ((), (), s32[]{:S(2)}) async-start(), calls=%async_computation.11 | async-start | bytes 2359296 | tf_op jit(solution)/shard_map/all_gather | solution.py:58
  105.1 135.9 %all-gather.8.cloned.1.call-start = ((), (), s32[]{:S(2)}) async-start(), calls=%async_computation.12 | async-start | bytes 2359296 | tf_op jit(solution)/shard_map/all_gather | solution.py:59
  105.7 176.8 %all-reduce.9.cloned.1.call-start = ((), (), s32[]{:S(2)}) async-start(), calls=%async_computation.14 | async-start | bytes 2097152 | tf_op jit(solution)/shard_map/psum | solution.py:142
  141.3 177.8 %copy-start.25 = (f32[256]{0:T(256)}, f32[256]{0:T(256)S(1)}, u32[]{:S(2)}) copy-start(f32[256]{0:T(256)S(1)} %add_rsqrt_fusion) | copy-start | bytes 3076
  241.0 4.7 copy-start.10
  244.9 0.8 copy-start.11
  247.5 71.6 %all-reduce.7.cloned.1.call-start = ((), (), s32[]{:S(2)}) async-start(), calls=%async_computation.13 | async-start | bytes 1048576 | tf_op jit(solution)/shard_map/psum | solution.py:123
  251.1 90.2 %reduce-scatter.18.cloned.1.call-start = ((), (), s32[]{:S(2)}) async-start(), calls=%async_computation.16 | async-start | bytes 786432 | tf_op jit(solution)/shard_map/reduce_scatter | solution.py:175
  319.1 4.0 copy-start.4
  322.1 1.0 copy-start.1
  326.3 31.8 %reduce-scatter.16.cloned.1.call-start = ((), (), s32[]{:S(2)}) async-start(), calls=%async_computation.15 | async-start | bytes 786432 | tf_op jit(solution)/shard_map/reduce_scatter | solution.py:174
  326.4 3.3 copy-start.13
  328.9 0.8 copy-start.5
  330.7 68.0 %all-reduce.11.cloned.1.call-start = ((), (), s32[]{:S(2)}) async-start(), calls=%async_computation.17 | async-start | bytes 2097152 | tf_op jit(solution)/shard_map/psum | solution.py:191
  359.2 3.1 copy-start.27
  362.3 102.8 %reduce-scatter.32.cloned.1.call-start = ((), (), s32[]{:S(2)}) async-start(), calls=%async_computation.24 | async-start | bytes 589824
  362.3 41.3 %copy-start.17 = (f32[1024]{0:T(1024)S(1)}, f32[1024]{0:T(1024)}, u32[]{:S(2)}) copy-start(f32[1024]{0:T(1024)} %get-tuple-element.38) | copy-start | bytes 12292
  363.4 43.3 %copy-start.8 = (f32[256,1024]{1,0:T(8,128)S(1)}, f32[256,1024]{1,0:T(8,128)}, u32[]{:S(2)}) copy-start(f32[256,1024]{1,0:T(8,128)} %convolution_add_fusion) | copy-start | bytes 3145732
  363.4 166.6 %reduce-scatter.30.cloned.1.call-start = ((), (), s32[]{:S(2)}) async-start(), calls=%async_computation.23 | async-start | bytes 589824
  398.7 2.5 copy-start.18
  403.5 191.8 %reduce-scatter.28.cloned.1.call-start = ((), (), s32[]{:S(2)}) async-start(), calls=%async_computation.22 | async-start | bytes 589824
  406.6 280.0 %reduce-scatter.26.cloned.1.call-start = ((), (), s32[]{:S(2)}) async-start(), calls=%async_computation.21 | async-start | bytes 4718592 | tf_op jit(solution)/shard_map/reduce_scatter | solution.py:203
  410.6 1.2 copy-start.2
  410.6 343.9 %reduce-scatter.22.cloned.1.call-start = ((), (), s32[]{:S(2)}) async-start(), calls=%async_computation.19 | async-start | bytes 1179648 | tf_op jit(solution)/shard_map/reduce_scatter | solution.py:201
  414.1 418.3 %reduce-scatter.20.cloned.1.call-start = ((), (), s32[]{:S(2)}) async-start(), calls=%async_computation.18 | async-start | bytes 3538944 | tf_op jit(solution)/shard_map/reduce_scatter | solution.py:200
  417.5 0.7 copy-start.20
  417.5 0.7 copy-start.26
  417.6 506.4 %reduce-scatter.24.cloned.1.call-start = ((), (), s32[]{:S(2)}) async-start(), calls=%async_computation.20 | async-start | bytes 4718592 | tf_op jit(solution)/shard_map/reduce_scatter | solution.py:202
  422.1 44.3 %copy-start.30 = (f32[256]{0:T(256)S(1)}, f32[256]{0:T(256)}, u32[]{:S(2)}) copy-start(f32[256]{0:T(256)} %get-tuple-element.37) | copy-start | bytes 3076
  422.1 44.3 %copy-start.29 = (f32[256]{0:T(256)S(1)}, f32[256]{0:T(256)}, u32[]{:S(2)}) copy-start(f32[256]{0:T(256)} %get-tuple-element.41) | copy-start | bytes 3076
  422.1 44.3 %copy-start.7 = (f32[256,1024]{1,0:T(8,128)S(1)}, f32[256,1024]{1,0:T(8,128)}, u32[]{:S(2)}) copy-start(f32[256,1024]{1,0:T(8,128)} %all-reduce.11.cloned.1.call-done) | copy-start | bytes 3145732
  422.1 44.3 %copy-start.22 = (f32[256]{0:T(256)S(1)}, f32[256]{0:T(256)}, u32[]{:S(2)}) copy-start(f32[256]{0:T(256)} %copy-done.21) | copy-start | bytes 3076
  422.1 44.4 %copy-start.24 = (f32[256]{0:T(256)S(1)}, f32[256]{0:T(256)}, u32[]{:S(2)}) copy-start(f32[256]{0:T(256)} %copy-done.23) | copy-start | bytes 3076
Sparse Core Ops, SparseCore 0:
  10.2 47.6 all-gather.3
  104.5 35.1 all-reduce.4
  141.8 49.5 all-gather.5
  193.3 47.6 all-gather.7
  247.6 34.8 all-reduce.8
  285.2 33.8 all-reduce.6
  326.5 14.7 reduce-scatter.17
  343.5 14.6 reduce-scatter.15
  362.4 36.2 all-reduce.10
  401.9 63.0 reduce-scatter.31
  468.4 61.5 reduce-scatter.29
  533.7 61.5 reduce-scatter.27
  599.0 87.6 reduce-scatter.25
  690.5 63.9 reduce-scatter.21
  758.5 73.8 reduce-scatter.19
  836.5 87.4 reduce-scatter.23
where the time goes:
time: 932 us; the launch traced here: 930 us
  waiting for transfers between devices  731 us (78%)
  blocking collectives  105 us (11%)
  matrix products  38.5 us (4%)
  other arithmetic  21.5 us (2%)
  local copies, waits for them, and re-layouts  19.6 us (2%)
  between operations  14.5 us (2%)
    unnamed x19, waiting for transfers between devices  171 us
    reduce_scatter x1, waiting for transfers between devices, shards(): lax.psum_scatter(expand_grad, ('shard', 'ctx'), scatter_dimension=0, tile...  91.5 us
    reduce_scatter x1, waiting for transfers between devices, shards(): lax.psum_scatter(reduce_grad, ('shard', 'ctx'), scatter_dimension=0, tile...  89.8 us
    reduce_scatter x1, waiting for transfers between devices, shards(): lax.psum_scatter(attend_grad, ('shard', 'ctx'), scatter_dimension=0, tile...  78 us
    reduce_scatter x1, waiting for transfers between devices, shards(): lax.psum_scatter(merge_grad, ('shard', 'ctx'), scatter_dimension=0, tiled...  65.8 us
    all_gather x1, waiting for transfers between devices, shards(): lax.all_gather(expand_weight, ('shard', 'ctx'), axis=0, tiled=True)  50 us
    all_gather x1, waiting for transfers between devices, shards(): lax.all_gather(reduce_weight, ('shard', 'ctx'), axis=0, tiled=True)  46.3 us
    psum x1, waiting for transfers between devices, shards(): early_grad = lax.psum(early_part, 'tp')  35.1 us
  transfers between devices with their start and end apart: 16, of which 15 were waited for; matrix products, arithmetic and copies ran while one was open for 6% of the time, Pallas kernels for 0%

commit v1 on v0

--- a/solution.py
+++ b/solution.py
@@ -139,7 +139,7 @@
         "rd,rf->df", hidden_later, pre_half, preferred_element_type=jnp.float32
     )
     later_part = jnp.einsum("rf,df->rd", pre_half, expand_back, preferred_element_type=jnp.float32)
-    later_grad = lax.psum(later_part, "tp")
+    later_grad = lax.all_gather(later_part, axis_name="tp").sum(axis=0)
     residual_grad = output_grad + norm_backward(
         later_grad, normed_later, inverse_later, gains_back[1]
     )

time: 932 us -> 930 us (level)
    psum x1 -> x0, waiting for transfers between devices: 31.3 us -> none  [shards(): later_grad = lax.psum(later_part, 'tp')]
    all_gather x0 -> x1, waiting for transfers between devices: none -> 29.5 us  [shards(): later_grad = lax.all_gather(later_part, axis_name='tp').sum(axis=0)]
where the time goes in v1:
time: 930 us; the launch traced here: 928 us
  waiting for transfers between devices  723 us (78%)
  blocking collectives  105 us (11%)
  matrix products  37.5 us (4%)
  other arithmetic  28.2 us (3%)
  local copies, waits for them, and re-layouts  19.9 us (2%)
  between operations  14.5 us (2%)
    unnamed x19, waiting for transfers between devices  172 us
    reduce_scatter x1, waiting for transfers between devices, shards(): lax.psum_scatter(expand_grad, ('shard', 'ctx'), scatter_dimension=0, tile...  91.4 us
    reduce_scatter x1, waiting for transfers between devices, shards(): lax.psum_scatter(reduce_grad, ('shard', 'ctx'), scatter_dimension=0, tile...  89.8 us
    reduce_scatter x1, waiting for transfers between devices, shards(): lax.psum_scatter(attend_grad, ('shard', 'ctx'), scatter_dimension=0, tile...  78.4 us
    reduce_scatter x1, waiting for transfers between devices, shards(): lax.psum_scatter(merge_grad, ('shard', 'ctx'), scatter_dimension=0, tiled...  65.6 us
    all_gather x1, waiting for transfers between devices, shards(): lax.all_gather(expand_weight, ('shard', 'ctx'), axis=0, tiled=True)  50 us
    all_gather x1, waiting for transfers between devices, shards(): lax.all_gather(reduce_weight, ('shard', 'ctx'), axis=0, tiled=True)  46.3 us
    psum x1, waiting for transfers between devices, shards(): early_grad = lax.psum(early_part, 'tp')  32 us
  transfers between devices with their start and end apart: 16, of which 15 were waited for; matrix products, arithmetic and copies ran while one was open for 6% of the time, Pallas kernels for 0%

profile of v1, /device:TPU:0, one launch (start us, length us, event | category | flops | bytes accessed | tf_op | source)
XLA Modules:
  0.0 928.4 jit_solution(8659205784292904864)
XLA Ops:
  8.0 1.4 reduce_sum.135
  9.4 5.5 all_gather.45
  14.8 21.4 %all_gather.41 = bf16[2,1024]{1,0:T(2,128)(2,1)S(1)} all-gather(bf16[2,128]{1,0:T(2,128)(2,1)} %param.12), channel_id=1, replica_groups=mesh['shard'=4,'ctx'=2,'tp'=4] {'shard','ctx'}, dimensions={1}, use_global_device_ids=true | all-gather | bytes 4608 | tf_op jit(solution)/shard_map/all_gather | solution.py:61
  36.3 16.5 %all_gather.42 = bf16[2,1024]{1,0:T(2,128)(2,1)S(1)} all-gather(bf16[2,128]{1,0:T(2,128)(2,1)} %param.13), channel_id=1, replica_groups=mesh['shard'=4,'ctx'=2,'tp'=4] {'shard','ctx'}, dimensions={1}, use_global_device_ids=true | all-gather | bytes 4608 | tf_op jit(solution)/shard_map/all_gather | solution.py:62
  52.8 1.5 multiply_reduce_fusion.5
  54.6 31.4 %all_gather.47 = bf16[1024,256]{1,0:T(8,128)(2,1)S(1)} all-gather(bf16[128,256]{1,0:T(8,128)(2,1)S(1)} %copy-done.17), channel_id=1, replica_groups=mesh['shard'=4,'ctx'=2,'tp'=4] {'shard','ctx'}, dimensions={0}, use_global_device_ids=true | all-gather | bytes 589824 | tf_op jit(solution)/shard_map/all_gather | solution.py:57
  86.3 2.1 fusion.38
  88.5 5.6 all_gather.44
  95.0 5.6 all_gather.46
  105.7 18.4 %all_gather.49 = bf16[1,1024]{1,0:T(2,128)(2,1)S(1)} all-gather(bf16[1,128]{1,0:T(2,128)(2,1)S(1)} %copy-done.31), channel_id=1, replica_groups=mesh['shard'=4,'ctx'=2,'tp'=4] {'shard','ctx'}, dimensions={1}, use_global_device_ids=true | all-gather | bytes 2304 | tf_op jit(solution)/shard_map/all_gather | solution.py:60
  124.1 2.1 bitcast_convert_fusion
  126.2 13.4 %all-reduce.4.cloned.1.call-done = f32[256,1024]{1,0:T(8,128)} async-done(((f32[256,1024]{1,0:T(8,128)}), f32[256,1024]{1,0:T(8,128)}) %all-reduce.4.cloned.1.call-update) | async-done | bytes 1048592 | tf_op jit(solution)/shard_map/psum | solution.py:110
  139.6 1.4 fusion.36
  141.3 50.0 %all-gather.8.cloned.1.call-done = bf16[1024,1024]{1,0:T(8,128)(2,1)} async-done(((bf16[128,1024]{1,0:T(8,128)(2,1)}), bf16[1024,1024]{1,0:T(8,128)(2,1)}) %all-gather.8.cloned.1.call-update) | async-done | bytes 2097168 | tf_op jit(solution)/shard_map/all_gather | solution.py:58
  191.4 3.3 convolution_add_fusion
  194.7 46.3 %all-gather.10.cloned.1.call-done = bf16[1024,1024]{1,0:T(8,128)(2,1)} async-done(((bf16[128,1024]{1,0:T(8,128)(2,1)}), bf16[1024,1024]{1,0:T(8,128)(2,1)}) %all-gather.10.cloned.1.call-update) | async-done | bytes 2097168 | tf_op jit(solution)/shard_map/all_gather | solution.py:59
  241.0 3.9 fusion.40
  245.8 1.7 fusion.21
  247.6 3.5 convolution_convert_fusion
  251.2 29.5 %all-gather.12.cloned.1.call-done = f32[1024,1024]{1,0:T(8,128)} async-done(((f32[256,1024]{1,0:T(8,128)}), f32[1024,1024]{1,0:T(8,128)}) %all-gather.12.cloned.1.call-update) | async-done | bytes 4194320 | tf_op jit(solution)/shard_map/all_gather | solution.py:142
  280.6 3.7 reduce_sum.140
  284.3 2.3 multiply_reduce_fusion
  286.6 30.2 %all-reduce.6.cloned.1.call-done = bf16[256,1024]{1,0:T(8,128)(2,1)} async-done(((bf16[256,1024]{1,0:T(8,128)(2,1)}), bf16[256,1024]{1,0:T(8,128)(2,1)}) %all-reduce.6.cloned.1.call-update) | async-done | bytes 524304 | tf_op jit(solution)/shard_map/psum | solution.py:123
  316.9 3.0 bitcast_add_fusion
  325.2 1.4 fusion.1
  330.3 8.6 reduce-scatter.18.cloned.1.call-done
  340.1 15.8 %reduce-scatter.16.cloned.1.call-done = f32[2,128,256]{1,2,0:T(8,128)} async-done(((f32[2,256,256]{1,2,0:T(8,128)}), f32[2,128,256]{1,2,0:T(8,128)}) %reduce-scatter.16.cloned.1.call-update) | async-done | bytes 262160 | tf_op jit(solution)/shard_map/reduce_scatter | solution.py:174
  357.0 3.0 convolution_bitcast_fusion.1
  361.4 3.1 reduce_sum.148
  364.4 32.0 %all-reduce.8.cloned.1.call-done = f32[256,1024]{1,0:T(8,128)} async-done(((f32[256,1024]{1,0:T(8,128)}), f32[256,1024]{1,0:T(8,128)}) %all-reduce.8.cloned.1.call-update) | async-done | bytes 1048592 | tf_op jit(solution)/shard_map/psum | solution.py:191
  396.5 2.5 multiply_reduce_fusion.1
  399.5 1.7 copy.70
  402.6 1.7 copy.68
  404.4 3.9 convolution_bitcast_fusion
  409.5 2.3 fusion.16
  411.9 3.9 fusion.19
  416.8 2.4 fusion.11
  419.2 43.6 %reduce-scatter.32.cloned.1.call-done = f32[128,1]{1,0:T(8,128)} async-done(((f32[1024,1]{1,0:T(8,128)}), f32[128,1]{1,0:T(8,128)}) %reduce-scatter.32.cloned.1.call-update) | async-done | bytes 528
  462.8 1.4 copy.73
  465.6 62.2 %reduce-scatter.30.cloned.1.call-done = f32[128,2]{1,0:T(8,128)} async-done(((f32[1024,2]{1,0:T(8,128)}), f32[128,2]{1,0:T(8,128)}) %reduce-scatter.30.cloned.1.call-update) | async-done | bytes 1040
  527.8 1.5 copy.71
  529.2 63.9 %reduce-scatter.28.cloned.1.call-done = f32[128,2]{1,0:T(8,128)} async-done(((f32[1024,2]{1,0:T(8,128)}), f32[128,2]{1,0:T(8,128)}) %reduce-scatter.28.cloned.1.call-update) | async-done | bytes 1040
  593.2 1.5 copy.69
  594.6 89.8 %reduce-scatter.26.cloned.1.call-done = f32[128,1024]{0,1:T(8,128)} async-done(((f32[1024,1024]{0,1:T(8,128)}), f32[128,1024]{0,1:T(8,128)}) %reduce-scatter.26.cloned.1.call-update) | async-done | bytes 524304 | tf_op jit(solution)/shard_map/reduce_scatter | solution.py:203
  684.5 2.0 copy.58
  686.5 65.6 %reduce-scatter.22.cloned.1.call-done = f32[128,256]{1,0:T(8,128)} async-done(((f32[1024,256]{1,0:T(8,128)}), f32[128,256]{1,0:T(8,128)}) %reduce-scatter.22.cloned.1.call-update) | async-done | bytes 131088 | tf_op jit(solution)/shard_map/reduce_scatter | solution.py:201
  752.1 91.4 %reduce-scatter.24.cloned.1.call-done = f32[128,1024]{1,0:T(8,128)} async-done(((f32[1024,1024]{1,0:T(8,128)}), f32[128,1024]{1,0:T(8,128)}) %reduce-scatter.24.cloned.1.call-update) | async-done | bytes 524304 | tf_op jit(solution)/shard_map/reduce_scatter | solution.py:202
  843.6 78.4 %reduce-scatter.20.cloned.1.call-done = f32[128,3,256]{2,0,1:T(8,128)} async-done(((f32[1024,3,256]{2,0,1:T(8,128)}), f32[128,3,256]{2,0,1:T(8,128)}) %reduce-scatter.20.cloned.1.call-update) | async-done | bytes 393232 | tf_op jit(solution)/shard_map/reduce_scatter | solution.py:200
  (142 shorter events, 26.4 us)
Async XLA Ops:
  7.2 78.8 %copy-start = (f32[2,128,1024]{2,1,0:T(8,128)S(1)}, f32[2,128,1024]{2,1,0:T(8,128)}, u32[]{:S(2)}) copy-start(f32[2,128,1024]{2,1,0:T(8,128)} %param.10) | copy-start | bytes 3145732
  7.2 47.3 %copy-start.28 = (s32[2,128]{1,0:T(2,128)S(1)}, s32[2,128]{1,0:T(2,128)}, u32[]{:S(2)}) copy-start(s32[2,128]{1,0:T(2,128)} %param.11) | copy-start | bytes 3076
  7.2 47.4 %copy-start.17 = (bf16[128,256]{1,0:T(8,128)(2,1)S(1)}, bf16[128,256]{1,0:T(8,128)(2,1)}, u32[]{:S(2)}) copy-start(bf16[128,256]{1,0:T(8,128)(2,1)} %param.15) | copy-start | bytes 196612
  7.2 79.1 %all-gather.6.cloned.1.call-start = ((), (), s32[]{:S(2)}) async-start(), calls=%async_computation.9 | async-start | bytes 1769472 | tf_op jit(solution)/shard_map/all_gather | solution.py:56
  7.9 131.7 %all-reduce.4.cloned.1.call-start = ((), (), s32[]{:S(2)}) async-start(), calls=%async_computation.10 | async-start | bytes 2097152 | tf_op jit(solution)/shard_map/psum | solution.py:110
  52.8 35.6 %copy-start.22 = (f32[256]{0:T(256)}, f32[256]{0:T(256)S(1)}, u32[]{:S(2)}) copy-start(f32[256]{0:T(256)S(1)} %get-tuple-element.53) | copy-start | bytes 3076
  54.3 34.1 %copy-start.24 = (f32[256]{0:T(256)}, f32[256]{0:T(256)S(1)}, u32[]{:S(2)}) copy-start(f32[256]{0:T(256)S(1)} %rsqrt_bitcast_fusion) | copy-start | bytes 3076
  54.4 137.0 %copy-start.20 = (f32[1,1024]{1,0:T(1,128)}, f32[1,1024]{1,0:T(1,128)S(1)}, u32[]{:S(2)}) copy-start(f32[1,1024]{1,0:T(1,128)S(1)} %get-tuple-element.51) | copy-start | bytes 12292
  86.0 16.5 %copy-start.3 = (bf16[1024,256]{1,0:T(8,128)(2,1)}, bf16[1024,256]{1,0:T(8,128)(2,1)S(1)}, u32[]{:S(2)}) copy-start(bf16[1024,256]{1,0:T(8,128)(2,1)S(1)} %all_gather.47) | copy-start | bytes 1572868
  86.2 7.9 copy-start.6
  100.6 1.3 copy-start.10
  101.1 1.4 copy-start.13
  102.3 0.7 copy-start.16
  102.3 3.4 copy-start.31
  102.5 23.7 %copy-start.15 = (bf16[2,128,4,64]{1,0,3,2:T(2,128)(2,1)}, bf16[2,128,4,64]{1,0,3,2:T(2,128)(2,1)S(1)}, u32[]{:S(2)}) copy-start(bf16[2,128,4,64]{1,0,3,2:T(2,128)(2,1)S(1)} %copy.48) | copy-start | bytes 393220
  104.3 87.0 %all-gather.8.cloned.1.call-start = ((), (), s32[]{:S(2)}) async-start(), calls=%async_computation.11 | async-start | bytes 2359296 | tf_op jit(solution)/shard_map/all_gather | solution.py:58
  105.1 135.9 %all-gather.10.cloned.1.call-start = ((), (), s32[]{:S(2)}) async-start(), calls=%async_computation.12 | async-start | bytes 2359296 | tf_op jit(solution)/shard_map/all_gather | solution.py:59
  105.6 175.0 %all-gather.12.cloned.1.call-start = ((), (), s32[]{:S(2)}) async-start(), calls=%async_computation.21 | async-start | bytes 5242880 | tf_op jit(solution)/shard_map/all_gather | solution.py:142
  141.3 175.6 %copy-start.26 = (f32[256]{0:T(256)}, f32[256]{0:T(256)S(1)}, u32[]{:S(2)}) copy-start(f32[256]{0:T(256)S(1)} %add_rsqrt_fusion) | copy-start | bytes 3076
  241.0 4.8 copy-start.11
  244.9 0.8 copy-start.12
  247.5 69.3 %all-reduce.6.cloned.1.call-start = ((), (), s32[]{:S(2)}) async-start(), calls=%async_computation.13 | async-start | bytes 1048576 | tf_op jit(solution)/shard_map/psum | solution.py:123
  251.1 87.9 %reduce-scatter.18.cloned.1.call-start = ((), (), s32[]{:S(2)}) async-start(), calls=%async_computation.15 | async-start | bytes 786432 | tf_op jit(solution)/shard_map/reduce_scatter | solution.py:175
  316.9 4.0 copy-start.4
  319.9 1.0 copy-start.1
  324.1 31.8 %reduce-scatter.16.cloned.1.call-start = ((), (), s32[]{:S(2)}) async-start(), calls=%async_computation.14 | async-start | bytes 786432 | tf_op jit(solution)/shard_map/reduce_scatter | solution.py:174
  324.1 3.3 copy-start.14
  326.6 0.8 copy-start.5
  328.5 67.9 %all-reduce.8.cloned.1.call-start = ((), (), s32[]{:S(2)}) async-start(), calls=%async_computation.16 | async-start | bytes 2097152 | tf_op jit(solution)/shard_map/psum | solution.py:191
  357.0 3.1 copy-start.27
  360.0 102.7 %reduce-scatter.32.cloned.1.call-start = ((), (), s32[]{:S(2)}) async-start(), calls=%async_computation.24 | async-start | bytes 589824
  361.1 166.6 %reduce-scatter.30.cloned.1.call-start = ((), (), s32[]{:S(2)}) async-start(), calls=%async_computation.23 | async-start | bytes 589824
  364.4 36.9 %copy-start.18 = (f32[1024]{0:T(1024)S(1)}, f32[1024]{0:T(1024)}, u32[]{:S(2)}) copy-start(f32[1024]{0:T(1024)} %get-tuple-element.38) | copy-start | bytes 12292
  364.4 40.0 %copy-start.9 = (f32[256,1024]{1,0:T(8,128)S(1)}, f32[256,1024]{1,0:T(8,128)}, u32[]{:S(2)}) copy-start(f32[256,1024]{1,0:T(8,128)} %convolution_add_fusion) | copy-start | bytes 3145732
  396.5 2.5 copy-start.19
  401.3 191.9 %reduce-scatter.28.cloned.1.call-start = ((), (), s32[]{:S(2)}) async-start(), calls=%async_computation.22 | async-start | bytes 589824
  404.4 280.1 %reduce-scatter.26.cloned.1.call-start = ((), (), s32[]{:S(2)}) async-start(), calls=%async_computation.20 | async-start | bytes 4718592 | tf_op jit(solution)/shard_map/reduce_scatter | solution.py:203
  408.3 1.2 copy-start.2
  408.3 3.5 copy-start.21
  408.3 343.8 %reduce-scatter.22.cloned.1.call-start = ((), (), s32[]{:S(2)}) async-start(), calls=%async_computation.18 | async-start | bytes 1179648 | tf_op jit(solution)/shard_map/reduce_scatter | solution.py:201
  411.8 431.7 %reduce-scatter.24.cloned.1.call-start = ((), (), s32[]{:S(2)}) async-start(), calls=%async_computation.19 | async-start | bytes 4718592 | tf_op jit(solution)/shard_map/reduce_scatter | solution.py:202
  415.8 1.0 copy-start.7
  415.8 506.1 %reduce-scatter.20.cloned.1.call-start = ((), (), s32[]{:S(2)}) async-start(), calls=%async_computation.17 | async-start | bytes 3538944 | tf_op jit(solution)/shard_map/reduce_scatter | solution.py:200
  419.2 45.0 %copy-start.30 = (f32[256]{0:T(256)S(1)}, f32[256]{0:T(256)}, u32[]{:S(2)}) copy-start(f32[256]{0:T(256)} %get-tuple-element.37) | copy-start | bytes 3076
  419.2 45.0 %copy-start.29 = (f32[256]{0:T(256)S(1)}, f32[256]{0:T(256)}, u32[]{:S(2)}) copy-start(f32[256]{0:T(256)} %get-tuple-element.41) | copy-start | bytes 3076
  419.2 45.0 %copy-start.8 = (f32[256,1024]{1,0:T(8,128)S(1)}, f32[256,1024]{1,0:T(8,128)}, u32[]{:S(2)}) copy-start(f32[256,1024]{1,0:T(8,128)} %all-reduce.8.cloned.1.call-done) | copy-start | bytes 3145732
  419.2 45.1 %copy-start.23 = (f32[256]{0:T(256)S(1)}, f32[256]{0:T(256)}, u32[]{:S(2)}) copy-start(f32[256]{0:T(256)} %copy-done.22) | copy-start | bytes 3076
  419.2 45.1 %copy-start.25 = (f32[256]{0:T(256)S(1)}, f32[256]{0:T(256)}, u32[]{:S(2)}) copy-start(f32[256]{0:T(256)} %copy-done.24) | copy-start | bytes 3076
Sparse Core Ops, SparseCore 0:
  10.2 47.6 all-gather.5
  104.5 35.1 all-reduce.3
  141.8 49.5 all-gather.7
  193.3 47.6 all-gather.9
  247.6 32.9 all-gather.11
  283.4 33.3 all-reduce.5
  324.2 14.7 reduce-scatter.17
  341.2 14.6 reduce-scatter.15
  360.1 36.2 all-reduce.7
  399.7 63.0 reduce-scatter.31
  466.1 61.5 reduce-scatter.29
  531.5 61.5 reduce-scatter.27
  596.8 87.6 reduce-scatter.25
  688.3 63.7 reduce-scatter.21
  756.2 87.3 reduce-scatter.23
  847.6 74.2 reduce-scatter.19
